TPU v7x, 32 devices: a whole 2x2x4 slice. The times are simulated.
32 devices in a mesh: groups: 2 (over y), panels: 4 (over z), cols: 2 (over x), phase: 2 (over core).
Axes of the slice: x: 2, y: 2, z: 4, core: 2. Of those that a mesh axis runs over, the one named last changes fastest.
Arguments:
- base_points: float32 [3, 512], P(None, ('groups', 'panels', 'cols')), parts along dimension 1, may hold values from -6 to 6
- control_points: float32 [3, 2048], replicated, may hold values from -6 to 6
- morph_weights: float32 [4, 3, 2048], P('groups'), parts along dimension 0, may hold values from -0.15 to 0.15
- connectivity: int32 [3, 1024], P(None, ('groups', 'panels', 'cols')), parts along dimension 1, may hold values from 0 to 255, as said below
- free_flags: int32 [1024], P(('groups', 'panels', 'cols')), parts along dimension 0, may hold values 0 or 1
- station_owner: int32 [1024, 1], P(('groups', 'panels', 'cols')), parts along dimension 0, may hold values from 0 to 7; in each aligned block of 64 rows (0 to 63, 64 to 127, ...) at most 20 rows name the same one
- variant_order: int32 [4], P('groups'), parts along dimension 0, may hold values from 0 to 1, each once
- load_velocity: float32 [64, 3], replicated, may hold values from -5 to 5
Outputs:
- shear: float32 [4, 64, 1024], P(('groups', 'phase'), None, ('panels', 'cols')), parts along dimension 0
- moment: float32 [4, 64, 1024], P(('groups', 'phase'), None, ('panels', 'cols')), parts along dimension 0
There are 2 independent parts, one for each index of `groups`. A program takes and returns all parts, laid end to end along the dimension named above; an argument that names none is the same for every part. Nothing has to cross between parts.
Inputs may be any that keep to these rules, and one draw needn't show every extreme that they name: `connectivity`: the vertices of panel i lie in block i // 64 of 32 consecutive vertices: from (i // 64) * 32 to (i // 64 + 1) * 32 - 1. `station_owner`: among the panels of one device (aligned blocks of 64 panels) no station owner is named more than 20 times. `variant_order`: each variant appears once.
All inputs are finite; a program needn't handle non-finite values. No bound on the sum of `free_flags` on one device may be relied on, other than what follows from the above.
Results may differ from a plain program's by a relative error of at most 0.0015.
Values may be sent and summed in bfloat16 or wider, within the bound.
A program may use at most 64 MiB of HBM per device.

v0:
```python
import math

import jax
import jax.numpy as jnp
from jax import lax
from jax.sharding import PartitionSpec as P

STATIONS = 128


HIGH = lax.Precision.HIGHEST
CORE_SQUARE = 0.0025
SKIN_SQUARE = 0.01


def prefix(shard, axis, combine, identity):
    length, index = (lax.axis_size(axis), lax.axis_index(axis))
    everything = jax.tree.map(lambda part: lax.all_gather(part, axis), shard)
    start = jax.tree.map(
        lambda part, zero: jnp.broadcast_to(jnp.asarray(zero, part.dtype), part.shape),
        shard,
        identity,
    )

    def step(k, before):
        reached = k < index
        new = combine(before, jax.tree.map(lambda part: part[k], everything))
        return jax.tree.map(lambda a, b: jnp.where(reached, a, b), new, before)

    return lax.fori_loop(0, length, step, start)


def panel_shape(moved_points, corner_rows):
    first_corner = jnp.take(moved_points, corner_rows[0], axis=2)
    second_corner = jnp.take(moved_points, corner_rows[1], axis=2)
    third_corner = jnp.take(moved_points, corner_rows[2], axis=2)
    centroid = (first_corner + second_corner + third_corner) / 3.0
    edge_one = second_corner - first_corner
    edge_two = third_corner - first_corner
    cross_x = edge_one[:, 1] * edge_two[:, 2] - edge_one[:, 2] * edge_two[:, 1]
    cross_y = edge_one[:, 2] * edge_two[:, 0] - edge_one[:, 0] * edge_two[:, 2]
    cross_z = edge_one[:, 0] * edge_two[:, 1] - edge_one[:, 1] * edge_two[:, 0]
    area = 0.5 * jnp.stack([cross_x, cross_y, cross_z], axis=1)
    weight = jnp.sqrt(jnp.sum(area * area, axis=1) + SKIN_SQUARE)
    return (centroid, area, weight)


def tile_block(targets, sources, strengths, kernel_scale):
    distance = (
        (targets[:, 0, :, None] - sources[:, 0, None, :]) ** 2
        + (targets[:, 1, :, None] - sources[:, 1, None, :]) ** 2
        + (targets[:, 2, :, None] - sources[:, 2, None, :]) ** 2
    )
    influence = (sources[:, 3, None, :] * kernel_scale * lax.rsqrt(distance + CORE_SQUARE)).astype(
        jnp.bfloat16
    )
    return jnp.einsum("mrn,mkn->mkr", influence, strengths, preferred_element_type=jnp.float32)


def tile_product(carry_sum, targets, sources, strengths, kernel_scale):
    columns = strengths.shape[2]
    block_width = columns
    for candidate in (2048, 1024, 512):
        if columns > candidate and columns % candidate == 0:
            block_width = candidate
            break
    if block_width == columns:
        return carry_sum + tile_block(targets, sources, strengths, kernel_scale)

    def block_step(step_index, running_sum):
        column_start = step_index * block_width
        part_sources = lax.dynamic_slice_in_dim(sources, column_start, block_width, 2)
        part_strengths = lax.dynamic_slice_in_dim(strengths, column_start, block_width, 2)
        return running_sum + tile_block(targets, part_sources, part_strengths, kernel_scale)

    return lax.fori_loop(0, columns // block_width, block_step, carry_sum)


def add_pairs(earlier, later):
    return (earlier[0] + later[0], earlier[1] + later[1])


def shards(
    base_points,
    control_points,
    morph_weights,
    connectivity,
    free_flags,
    station_owner,
    variant_order,
    load_velocity,
):
    owners = lax.axis_size(("panels", "cols"))
    owner_index = lax.axis_index(("panels", "cols"))
    phase_index = lax.axis_index("phase")
    variant_dev = variant_order.shape[0] // lax.axis_size("phase")
    vert_dev = base_points.shape[1]
    pan_dev = connectivity.shape[1]
    load_count = load_velocity.shape[0]
    panels_total = pan_dev * owners
    own_variants = lax.dynamic_slice_in_dim(
        variant_order, phase_index * variant_dev, variant_dev, 0
    )
    picker = (
        own_variants[:, None] == jnp.arange(variant_order.shape[0], dtype=jnp.int32)[None, :]
    ).astype(jnp.float32)
    chosen = jnp.einsum("mv,vac->mac", picker, morph_weights, precision=HIGH)
    distance = (
        (control_points[0][:, None] - base_points[0][None, :]) ** 2
        + (control_points[1][:, None] - base_points[1][None, :]) ** 2
        + (control_points[2][:, None] - base_points[2][None, :]) ** 2
    )
    basis_values = lax.rsqrt(1.0 + distance)
    moved_points = base_points[None] + jnp.einsum(
        "mac,cn->man", chosen, basis_values, precision=HIGH
    )
    local_corners = connectivity - owner_index * vert_dev
    centroid, area, weight = panel_shape(moved_points, local_corners)
    hull_mask = (1 - free_flags).astype(jnp.float32)
    boundary = (
        jnp.einsum("ka,man->mkn", load_velocity, area, precision=HIGH) * hull_mask[None, None, :]
    )
    first_strengths = boundary.astype(jnp.bfloat16)
    kernel_scale = 1.0 / (4.0 * math.pi * math.sqrt(panels_total))
    own_geometry = jnp.concatenate([centroid, weight[:, None, :]], axis=1)
    sources = lax.all_gather(own_geometry, "panels", axis=2, tiled=True)
    row_targets = lax.all_gather(centroid, "cols", axis=2, tiled=True)

    def apply_influence(strengths):
        empty_sum = jnp.zeros((variant_dev, load_count, row_targets.shape[2]), jnp.float32)
        partial_sums = tile_product(
            empty_sum,
            row_targets,
            sources,
            lax.all_gather(strengths, "panels", axis=2, tiled=True),
            kernel_scale,
        )
        return lax.psum_scatter(partial_sums, "cols", scatter_dimension=2, tiled=True)

    induced = apply_influence(first_strengths)
    second_strengths = (first_strengths.astype(jnp.float32) + (boundary - induced)).astype(
        jnp.bfloat16
    )
    pressure = apply_influence(second_strengths)
    panel_force = pressure * (area[:, 2, :] * hull_mask[None, :])[:, None, :]
    force_rows = panel_force.reshape(-1, pan_dev)
    capacity = max(2, 5 * pan_dev // (2 * owners))
    target_owner = station_owner[:, 0]
    panel_order = jnp.arange(pan_dev, dtype=jnp.int32)
    ahead = (target_owner[:, None] == target_owner[None, :]) & (
        panel_order[None, :] < panel_order[:, None]
    )
    slot_rank = jnp.sum(ahead.astype(jnp.int32), axis=1)
    slot_index = target_owner * capacity + slot_rank
    all_slots = jnp.arange(owners * capacity, dtype=jnp.int32)
    placed = slot_index[:, None] == all_slots[None, :]
    send_values = jnp.dot(force_rows, placed.astype(jnp.float32), precision=HIGH)
    station_bins = (owner_index * pan_dev + panel_order) % STATIONS
    send_bins = jnp.max(jnp.where(placed, station_bins[:, None], -1), axis=0)[None, :]
    recv_values, recv_bins = (
        lax.all_to_all(send_values, ("panels", "cols"), split_axis=1, concat_axis=1, tiled=True),
        lax.all_to_all(send_bins, ("panels", "cols"), split_axis=1, concat_axis=1, tiled=True),
    )
    matches = (recv_bins[0][:, None] == jnp.arange(STATIONS, dtype=jnp.int32)[None, :]).astype(
        jnp.float32
    )
    station_loads = jnp.dot(recv_values, matches, precision=HIGH)
    station_place = (owner_index * STATIONS + jnp.arange(STATIONS, dtype=jnp.int32)).astype(
        jnp.float32
    ) / (STATIONS * owners)
    placed_loads = station_loads * station_place[None, :]
    own_total = jnp.sum(station_loads, axis=1)
    own_arm = jnp.sum(placed_loads, axis=1)
    zero_row = jnp.zeros_like(own_total)
    prior_total, prior_arm = prefix(
        (own_total, own_arm), ("panels", "cols"), add_pairs, (zero_row, zero_row)
    )
    station_rank = jnp.arange(STATIONS, dtype=jnp.int32)
    inclusive = (station_rank[:, None] <= station_rank[None, :]).astype(jnp.float32)
    strict = (station_rank[:, None] < station_rank[None, :]).astype(jnp.float32)
    running = prior_total[:, None] + jnp.dot(station_loads, inclusive, precision=HIGH)
    earlier = prior_total[:, None] + jnp.dot(station_loads, strict, precision=HIGH)
    moment_arm = prior_arm[:, None] + jnp.dot(placed_loads, strict, precision=HIGH)
    inv_root = 1.0 / math.sqrt(panels_total)
    shear = (running * inv_root).reshape(variant_dev, load_count, STATIONS)
    moment = ((station_place[None, :] * earlier - moment_arm) * inv_root).reshape(
        variant_dev, load_count, STATIONS
    )
    return (shear, moment)


def solution(mesh):
    return jax.shard_map(
        shards,
        mesh=mesh,
        in_specs=(
            P(None, ("groups", "panels", "cols")),
            P(),
            P("groups", None, None),
            P(None, ("groups", "panels", "cols")),
            P(("groups", "panels", "cols")),
            P(("groups", "panels", "cols"), None),
            P("groups"),
            P(),
        ),
        out_specs=(
            P(("groups", "phase"), None, ("panels", "cols")),
            P(("groups", "phase"), None, ("panels", "cols")),
        ),
        check_vma=False,
    )
```

profile of v0, /device:TPU:0, one launch (start us, length us, event | category | flops | bytes accessed | tf_op | source)
XLA Modules:
  0.0 130.9 jit_solution(7332633443924360634)
XLA Ops:
  7.2 0.9 fusion.63
  9.4 0.9 fusion.48
  10.8 0.7 copy-done.1
  14.1 5.5 %all_gather.26 = f32[1,3,128]{1,2,0:T(8,128)S(1)} all-gather(f32[1,3,64]{1,2,0:T(8,128)S(1)} %get-tuple-element.175), channel_id=1, replica_groups=mesh['groups'=2,'panels'=4,'cols'=2,'phase'=2] {'cols'}, dimensions={2}, use_global_device_ids=true | all-gather | bytes 2304 | tf_op jit(solution)/shard_map/all_gather | solution.py:127
  19.6 14.1 %all_gather.25 = f32[1,4,256]{1,0,2:T(1,128)S(1)} all-gather(f32[1,4,64]{1,0,2:T(1,128)S(1)} %bitcast.124), channel_id=1, replica_groups=mesh['groups'=2,'panels'=4,'cols'=2,'phase'=2] {'panels'}, dimensions={2}, use_global_device_ids=true | all-gather | bytes 5120 | tf_op jit(solution)/shard_map/all_gather | solution.py:126
  33.8 3.3 %fusion.25 = (f32[256]{0:T(256)S(1)}, f32[256]{0:T(256)S(1)}, f32[256]{0:T(256)S(1)}, f32[256]{0:T(256)S(1)}) fusion(f32[1,4,256]{1,0,2:T(1,128)S(1)} %all_gather.25), kind=kLoop, calls=%fused_computation.44 | loop fusion | flops 256 | bytes 8192 | tf_op jit(solution)/shard_map/mul | solution.py:54
  37.1 0.7 copy-done.3
  38.1 13.2 %all_gather.24 = bf16[1,64,256]{1,2,0:T(8,128)(2,1)S(1)} all-gather(bf16[1,64,64]{1,2,0:T(8,128)(2,1)S(1)} %get-tuple-element.192), channel_id=1, replica_groups=mesh['groups'=2,'panels'=4,'cols'=2,'phase'=2] {'panels'}, dimensions={2}, use_global_device_ids=true | all-gather | bytes 40960 | tf_op jit(solution)/shard_map/all_gather | solution.py:135
  51.5 0.9 convolution_bitcast_fusion.1
  53.4 0.7 all_to_all.14
  54.1 5.7 %all-to-all-start.1 = ((s32[1,8,20]{2,0,1:T(1,128)}), s32[1,8,20]{2,0,1:T(1,128)S(1)}, u32[]{:S(2)}, u32[]{:S(2)}) async-start(s32[1,8,20]{2,0,1:T(1,128)} %all_to_all.14), calls=%async_computation.2 | async-start | bytes 8192 | tf_op jit(solution)/shard_map/all_to_all | solution.py:162
  61.8 1.9 %reduce-scatter.5.cloned.1.call-done = f32[1,64,64]{1,2,0:T(8,128)} async-done(((f32[1,64,128]{1,2,0:T(8,128)}), f32[1,64,64]{1,2,0:T(8,128)}) %reduce-scatter.5.cloned.1.call-update) | async-done | bytes 16400 | tf_op jit(solution)/shard_map/reduce_scatter | solution.py:138
  63.7 0.8 add_convert_fusion
  64.4 13.2 %all_gather.27 = bf16[1,64,256]{1,2,0:T(8,128)(2,1)S(1)} all-gather(bf16[1,64,64]{1,2,0:T(8,128)(2,1)S(1)} %add_convert_fusion), channel_id=1, replica_groups=mesh['groups'=2,'panels'=4,'cols'=2,'phase'=2] {'panels'}, dimensions={2}, use_global_device_ids=true | all-gather | bytes 40960 | tf_op jit(solution)/shard_map/all_gather | solution.py:135
  77.7 0.9 convolution_bitcast_fusion
  78.6 10.1 %reduce-scatter.7.cloned.1.call-done = f32[64,64]{1,0:T(8,128)} async-done(((f32[128,64]{1,0:T(8,128)}), f32[64,64]{1,0:T(8,128)}) %reduce-scatter.7.cloned.1.call-update) | async-done | bytes 16400
  88.7 0.8 copy.58
  89.7 0.7 reshape.458
  90.5 4.6 %all-to-all-start = ((f32[8,1,1280]{2,1,0:T(1,128)}), f32[8,1,1280]{2,1,0:T(1,128)S(1)}, u32[]{:S(2)}, u32[]{:S(2)}) async-start(f32[8,1,1280]{2,1,0:T(1,128)} %reshape.458), calls=%async_computation.1 | async-start | bytes 81920 | tf_op jit(solution)/shard_map/all_to_all | solution.py:161
  96.3 5.5 %all-to-all-done = f32[8,1,1280]{2,1,0:T(1,128)S(1)} async-done(((f32[8,1,1280]{2,1,0:T(1,128)}), f32[8,1,1280]{2,1,0:T(1,128)S(1)}, u32[]{:S(2)}, u32[]{:S(2)}) %all-to-all-start) | async-done | bytes 40992 | tf_op jit(solution)/shard_map/all_to_all | solution.py:161
  102.3 0.7 reduce.25
  104.0 17.8 %all-reduce.2 = (f32[512]{0:T(512)S(1)}, f32[512]{0:T(512)S(1)}) all-reduce(f32[512]{0:T(512)S(1)} %dynamic-update-slice, f32[512]{0:T(512)S(1)} %dynamic-update-slice.1), channel_id=2, replica_groups=mesh['groups'=2,'panels'=4,'cols'=2,'phase'=2] {'panels','cols'}, use_global_device_ids=true, to_apply=%add | all-reduce | flops 1024 | bytes 8192
  122.5 0.8 fusion.5
  123.3 0.8 fusion.2
  (76 shorter events, 10.9 us)
Async XLA Ops:
  7.2 2.2 %copy-start = (f32[2,3,2048]{2,0,1:T(2,128)S(1)}, f32[2,3,2048]{2,0,1:T(2,128)}, u32[]{:S(2)}) copy-start(f32[2,3,2048]{2,0,1:T(2,128)} %param.14) | copy-start | bytes 147460
  7.2 56.5 %reduce-scatter.5.cloned.1.call-start = ((), (), s32[]{:S(2)}) async-start(), calls=%async_computation.4 | async-start | bytes 98304 | tf_op jit(solution)/shard_map/reduce_scatter | solution.py:138
  7.2 0.9 copy-start.2
  8.2 0.7 copy-start.4
  10.8 0.7 copy-start.1
  33.8 3.3 %copy-start.6 = (s32[64]{0:T(128)S(1)}, s32[64]{0:T(128)}, u32[]{:S(2)}) copy-start(s32[64]{0:T(128)} %param.16) | copy-start | bytes 772
  37.1 0.7 copy-start.3
  52.4 0.7 copy-start.5
  54.1 36.4 %all-to-all-start.1 = ((s32[1,8,20]{2,0,1:T(1,128)}), s32[1,8,20]{2,0,1:T(1,128)S(1)}, u32[]{:S(2)}, u32[]{:S(2)}) async-start(s32[1,8,20]{2,0,1:T(1,128)} %all_to_all.14), calls=%async_computation.2 | async-start | bytes 8192 | tf_op jit(solution)/shard_map/all_to_all | solution.py:162
  59.7 28.9 %reduce-scatter.7.cloned.1.call-start = ((), (), s32[]{:S(2)}) async-start(), calls=%async_computation.5 | async-start | bytes 98304
  59.8 0.7 copy-start.7
  90.5 11.3 %all-to-all-start = ((f32[8,1,1280]{2,1,0:T(1,128)}), f32[8,1,1280]{2,1,0:T(1,128)S(1)}, u32[]{:S(2)}, u32[]{:S(2)}) async-start(f32[8,1,1280]{2,1,0:T(1,128)} %reshape.458), calls=%async_computation.1 | async-start | bytes 81920 | tf_op jit(solution)/shard_map/all_to_all | solution.py:161
Sparse Core Ops, SparseCore 0:
  52.5 11.1 reduce-scatter.4
  78.7 9.9 reduce-scatter.6
where the time goes:
time: 131 us
  blocking collectives  63.9 us (49%)
  waiting for transfers between devices  17.5 us (13%)
  between operations  15 us (11%)
  local copies, waits for them, and re-layouts  11.9 us (9%)
  starting transfers between devices  10.3 us (8%)
  other arithmetic  6.43 us (5%)
  matrix products  5.69 us (4%)
    all_gather x2, blocking collectives, apply_influence(): lax.all_gather(strengths, 'panels', axis=2, tiled=True)  26.4 us
    unnamed x1, blocking collectives  17.8 us
    all_gather x1, blocking collectives, shards(): sources = lax.all_gather(own_geometry, 'panels', axis=2, tiled=True)  14.1 us
    unnamed x3, waiting for transfers between devices  10.1 us
    unnamed x24, local copies, waits for them, and re-layouts  6.08 us
    all_to_all x1, starting transfers between devices, shards(): lax.all_to_all(send_bins, ('panels', 'cols'), split_axis=1, concat_axis=1...  5.66 us
    all_gather x1, blocking collectives, shards(): row_targets = lax.all_gather(centroid, 'cols', axis=2, tiled=True)  5.51 us
    all_to_all x1, waiting for transfers between devices, shards(): lax.all_to_all(send_values, ('panels', 'cols'), split_axis=1, concat_axis...  5.47 us
  transfers between devices with their start and end apart: 4, of which 3 were waited for; matrix products, arithmetic and copies ran while one was open for 4% of the time, Pallas kernels for 0%

commit v1 on v0

--- a/solution.py
+++ b/solution.py
@@ -1,8 +1,11 @@
+import functools
 import math
 
 import jax
 import jax.numpy as jnp
 from jax import lax
+from jax.experimental import pallas as pl
+from jax.experimental.pallas import tpu as pltpu
 from jax.sharding import PartitionSpec as P
 
 STATIONS = 128
@@ -189,9 +192,268 @@
     return (shear, moment)
 
 
+TILE_ROWS = 8
+LANES = 128
+FUSED_PANELS = 1024
+
+
+def own_geometry_rows(weights, points_col, corner_rows, control_ref, vert_dev):
+    controls = control_ref.shape[1]
+    chunk = min(controls, 2 * LANES)
+    totals = [jnp.zeros((vert_dev, chunk), jnp.float32) for _ in range(3)]
+    columns = [jnp.broadcast_to(col, (vert_dev, chunk)) for col in points_col]
+    for start in range(0, controls, chunk):
+        span = slice(start, start + chunk)
+        dx = control_ref[0:1, span] - columns[0]
+        dy = control_ref[1:2, span] - columns[1]
+        dz = control_ref[2:3, span] - columns[2]
+        basis = lax.rsqrt(1.0 + (dx * dx + dy * dy + dz * dz))
+        totals = [totals[a] + weights[a : a + 1, span] * basis for a in range(3)]
+    moved = [points_col[a] + jnp.sum(totals[a], axis=1, keepdims=True) for a in range(3)]
+    vertex = lax.broadcasted_iota(jnp.int32, (vert_dev, corner_rows.shape[1]), 0)
+    corners = []
+    for q in range(3):
+        hit = vertex == corner_rows[q : q + 1, :]
+        corners.append(
+            [jnp.sum(jnp.where(hit, moved[a], 0.0), axis=0, keepdims=True) for a in range(3)]
+        )
+    p0, p1, p2 = corners
+    centroid = [(p0[a] + p1[a] + p2[a]) / 3.0 for a in range(3)]
+    e1 = [p1[a] - p0[a] for a in range(3)]
+    e2 = [p2[a] - p0[a] for a in range(3)]
+    area = [
+        0.5 * (e1[1] * e2[2] - e1[2] * e2[1]),
+        0.5 * (e1[2] * e2[0] - e1[0] * e2[2]),
+        0.5 * (e1[0] * e2[1] - e1[1] * e2[0]),
+    ]
+    weight = jnp.sqrt(area[0] * area[0] + area[1] * area[1] + area[2] * area[2] + SKIN_SQUARE)
+    return centroid, weight, area
+
+
+def fused_kernel(
+    panels_axis,
+    cols_axis,
+    order_ref,
+    base_hbm,
+    control_hbm,
+    morph_hbm,
+    corner_hbm,
+    flag_hbm,
+    owner_hbm,
+    velocity_hbm,
+    shear_ref,
+    moment_ref,
+    base_ref,
+    control_ref,
+    morph_ref,
+    corner_ref,
+    flag_ref,
+    owner_ref,
+    velocity_ref,
+    mix_ref,
+    gathered,
+    influence_ref,
+    in_sem,
+    send_sem,
+    recv_sem,
+):
+    owners = panels_axis * cols_axis
+    row, col = lax.axis_index("panels"), lax.axis_index("cols")
+    me = row * cols_axis + col
+    vert_dev = base_ref.shape[1]
+    pan_dev = corner_ref.shape[1]
+    loads = velocity_ref.shape[1]
+    panels_total = pan_dev * owners
+
+    def peer_of(offset):
+        peer = lax.rem(me + offset, owners)
+        return {"panels": peer // cols_axis, "cols": lax.rem(peer, cols_axis)}
+
+    barrier = pltpu.get_barrier_semaphore()
+    for offset in range(1, owners):
+        pl.semaphore_signal(
+            barrier, inc=1, device_id=peer_of(offset), device_id_type=pl.DeviceIdType.MESH
+        )
+    pairs = (
+        (base_hbm, base_ref),
+        (control_hbm, control_ref),
+        (morph_hbm, morph_ref),
+        (corner_hbm, corner_ref),
+        (flag_hbm, flag_ref),
+        (owner_hbm, owner_ref),
+        (velocity_hbm, velocity_ref),
+    )
+    fetches = [
+        pltpu.make_async_copy(source, target, in_sem.at[k])
+        for k, (source, target) in enumerate(pairs)
+    ]
+    for fetch in fetches:
+        fetch.start()
+    mix_ref[...] = jnp.zeros(mix_ref.shape, jnp.float32)
+    for fetch in fetches:
+        fetch.wait()
+
+    mix_ref[0:3, 0:loads] = velocity_ref[...]
+    mix_ref[0:3, LANES : LANES + vert_dev] = base_ref[...]
+    mixed = mix_ref[...].T
+    velocity_col = [mixed[0:loads, a : a + 1] for a in range(3)]
+    points_col = [mixed[LANES : LANES + vert_dev, a : a + 1] for a in range(3)]
+    weights = morph_ref[order_ref[lax.axis_index("phase")]]
+    centroid, weight, area = own_geometry_rows(
+        weights, points_col, corner_ref[...] - me * vert_dev, control_ref, vert_dev
+    )
+    hull = (1 - flag_ref[...]).astype(jnp.float32)
+    station = (
+        owner_ref[...] * STATIONS
+        + lax.rem(me * pan_dev, STATIONS)
+        + lax.broadcasted_iota(jnp.int32, (1, pan_dev), 1)
+    ).astype(jnp.float32)
+    rows = centroid + [weight] + [part * hull for part in area] + [station]
+    gathered[me, :, 0:pan_dev] = jnp.concatenate(rows, axis=0)
+
+    pl.semaphore_wait(barrier, owners - 1)
+    sends = []
+    for offset in range(1, owners):
+        send = pltpu.make_async_remote_copy(
+            src_ref=gathered.at[me],
+            dst_ref=gathered.at[me],
+            send_sem=send_sem.at[offset - 1],
+            recv_sem=recv_sem.at[me],
+            device_id=peer_of(offset),
+            device_id_type=pl.DeviceIdType.MESH,
+        )
+        send.start()
+        sends.append(send)
+    for offset in range(1, owners):
+        source = lax.rem(me + offset, owners)
+        pltpu.make_async_remote_copy(
+            src_ref=gathered.at[source],
+            dst_ref=gathered.at[source],
+            send_sem=send_sem.at[offset - 1],
+            recv_sem=recv_sem.at[source],
+            device_id=peer_of(offset),
+            device_id_type=pl.DeviceIdType.MESH,
+        ).wait_recv()
+
+    rows = jnp.concatenate([gathered[d, :, 0:pan_dev] for d in range(owners)], axis=1)
+    columns = rows.T
+    kernel_scale = 1.0 / (4.0 * math.pi * math.sqrt(panels_total))
+    block = 32
+    for start in range(0, panels_total, block):
+        part = columns[start : start + block]
+        dx = rows[0:1] - part[:, 0:1]
+        dy = rows[1:2] - part[:, 1:2]
+        dz = rows[2:3] - part[:, 2:3]
+        distance = dx * dx + dy * dy + dz * dz
+        influence_ref[start : start + block, :] = (
+            (part[:, 3:4] * kernel_scale) * lax.rsqrt(distance + CORE_SQUARE)
+        ).astype(jnp.bfloat16)
+    boundary = (
+        velocity_col[0] * rows[4:5] + velocity_col[1] * rows[5:6] + velocity_col[2] * rows[6:7]
+    )
+    first = boundary.astype(jnp.bfloat16)
+    induced = jnp.dot(first, influence_ref[...], preferred_element_type=jnp.float32)
+    second = (first.astype(jnp.float32) + (boundary - induced)).astype(jnp.bfloat16)
+    pressure = jnp.dot(second, influence_ref[...], preferred_element_type=jnp.float32)
+    force = pressure * rows[6:7]
+    force_high = force.astype(jnp.bfloat16)
+    force_low = (force - force_high.astype(jnp.float32)).astype(jnp.bfloat16)
+    here = (
+        me * STATIONS + lax.broadcasted_iota(jnp.int32, (panels_total, STATIONS), 1)
+    ).astype(jnp.float32)
+    gap = here - columns[:, 7:8]
+    reached = jnp.where(gap >= 0.0, 1.0, 0.0).astype(jnp.bfloat16)
+    arm = jnp.maximum(gap, 0.0)
+    arm_high = arm.astype(jnp.bfloat16)
+    arm_low = (arm - arm_high.astype(jnp.float32)).astype(jnp.bfloat16)
+    summed = jnp.dot(
+        jnp.concatenate([force_high, force_low], axis=0),
+        jnp.concatenate([reached, arm_high, arm_low], axis=1),
+        preferred_element_type=jnp.float32,
+    )
+    summed = summed[0:loads] + summed[loads : 2 * loads]
+    inv_root = 1.0 / math.sqrt(panels_total)
+    shear_ref[0] = summed[:, 0:STATIONS] * inv_root
+    moment_ref[0] = (summed[:, STATIONS : 2 * STATIONS] + summed[:, 2 * STATIONS :]) * (
+        inv_root / (STATIONS * owners)
+    )
+    for send in sends:
+        send.wait_send()
+
+
+def fused_shards(
+    panels_axis,
+    cols_axis,
+    base_points,
+    control_points,
+    morph_weights,
+    connectivity,
+    free_flags,
+    station_owner,
+    variant_order,
+    load_velocity,
+):
+    owners = panels_axis * cols_axis
+    pan_dev = connectivity.shape[1]
+    loads = load_velocity.shape[0]
+    panels_total = pan_dev * owners
+    hbm_inputs = (
+        base_points,
+        control_points,
+        morph_weights,
+        connectivity,
+        free_flags.reshape(1, pan_dev),
+        station_owner.reshape(1, pan_dev),
+        load_velocity.T,
+    )
+    result = jax.ShapeDtypeStruct((1, loads, STATIONS), jnp.float32)
+    return tuple(
+        pl.pallas_call(
+            functools.partial(fused_kernel, panels_axis, cols_axis),
+            out_shape=(result, result),
+            in_specs=[pl.BlockSpec(memory_space=pltpu.SMEM)]
+            + [pl.BlockSpec(memory_space=pltpu.HBM)] * len(hbm_inputs),
+            out_specs=(pl.BlockSpec(memory_space=pltpu.VMEM),) * 2,
+            scratch_shapes=[pltpu.VMEM(part.shape, part.dtype) for part in hbm_inputs]
+            + [
+                pltpu.VMEM((TILE_ROWS, 2 * LANES), jnp.float32),
+                pltpu.VMEM((owners, TILE_ROWS, LANES), jnp.float32),
+                pltpu.VMEM((panels_total, panels_total), jnp.bfloat16),
+                pltpu.SemaphoreType.DMA((len(hbm_inputs),)),
+                pltpu.SemaphoreType.DMA((owners,)),
+                pltpu.SemaphoreType.DMA((owners,)),
+            ],
+            compiler_params=pltpu.CompilerParams(collective_id=0, has_side_effects=True),
+        )(variant_order, *hbm_inputs)
+    )
+
+
+def choose_shards(mesh, *arrays):
+    panels_axis, cols_axis = mesh.shape["panels"], mesh.shape["cols"]
+    owners = panels_axis * cols_axis
+    base_points, connectivity, variant_order, load_velocity = (
+        arrays[0],
+        arrays[3],
+        arrays[6],
+        arrays[7],
+    )
+    pan_dev = connectivity.shape[1]
+    fits = (
+        pan_dev * owners <= FUSED_PANELS
+        and pan_dev <= LANES
+        and STATIONS % pan_dev == 0
+        and base_points.shape[1] <= LANES
+        and load_velocity.shape[0] <= LANES
+        and variant_order.shape[0] == mesh.shape["phase"]
+    )
+    if fits:
+        return fused_shards(panels_axis, cols_axis, *arrays)
+    return shards(*arrays)
+
+
 def solution(mesh):
     return jax.shard_map(
-        shards,
+        functools.partial(choose_shards, mesh),
         mesh=mesh,
         in_specs=(
             P(None, ("groups", "panels", "cols")),

time: 131 us -> 16.2 us (0.12)
  blocking collectives: 63.9 us -> 0 us
  waiting for transfers between devices: 17.5 us -> 0 us
  between operations: 15 us -> 0.65 us
  Pallas kernels: 0 us -> 11.8 us
  starting transfers between devices: 10.3 us -> 0 us
  local copies, waits for them, and re-layouts: 11.9 us -> 3.45 us
  other arithmetic: 6.43 us -> 0 us
  matrix products: 5.69 us -> 0 us
    all_gather x4 -> x0, blocking collectives: 46.1 us -> none  [the longest x2 26.4 us: apply_influence(): lax.all_gather(strengths, 'panels', axis=2, tiled=True)]
    unnamed x1 -> x0, blocking collectives: 17.8 us -> none
    pallas_call x0 -> x1, Pallas kernels: none -> 11.8 us  [fused_shards(): pl.pallas_call(functools.partial(fused_kernel, panels_axis, cols_axis), o...]
    all_to_all x2 -> x0, starting transfers between devices: 10.2 us -> none  [the longest x1 5.66 us: shards(): lax.all_to_all(send_bins, ('panels', 'cols'), split_axis=1, concat_axis=1...]
    unnamed x3 -> x0, waiting for transfers between devices: 10.1 us -> none
    dot_general x10 -> x0, matrix products: 5.69 us -> none  [the longest x2 1.74 us: tile_block(): jnp.einsum('mrn,mkn->mkr', influence, strengths, preferred_element_type=j...]
    all_to_all x2 -> x0, waiting for transfers between devices: 5.48 us -> none  [the longest x1 5.47 us: shards(): lax.all_to_all(send_values, ('panels', 'cols'), split_axis=1, concat_axis...]
    mul x2 -> x0, other arithmetic: 3.33 us -> none  [the longest x1 3.33 us: tile_block(): sources[:, 3, None, :] * kernel_scale * lax.rsqrt(distance + CORE_SQUARE)]
  transfers between devices with their start and end apart: 4 -> 0, of which waited for: 3 -> 0; matrix products, arithmetic and copies ran while one was open for 4% -> 0% of each run, Pallas kernels for 0% -> 0%
where the time goes in v1:
time: 16.2 us; the launch traced here: 15.9 us
  Pallas kernels  11.8 us (73%)
  local copies, waits for them, and re-layouts  3.45 us (21%)
  between operations  0.65 us (4%)
    pallas_call x1, Pallas kernels, fused_shards(): pl.pallas_call(functools.partial(fused_kernel, panels_axis, cols_axis), o...  11.8 us
    unnamed x5, local copies, waits for them, and re-layouts  3.45 us

profile of v1, /device:TPU:0, one launch (start us, length us, event | category | flops | bytes accessed | tf_op | source)
XLA Modules:
  0.0 15.9 jit_solution(8482448834055934497)
XLA Ops:
  0.6 1.4 %copy.10.morph_hbm = f32[2,3,2048]{2,1,0:T(4,128)} copy(f32[2,3,2048]{2,0,1:T(2,128)} %param.10) | data formatting | bytes 98304 | tf_op args[2]
  2.1 11.8 %shard_map.95 = (f32[1,64,128]{2,1,0:T(8,128)}, f32[1,64,128]{2,1,0:T(8,128)}) custom-call(s32[2]{0:T(128)} %order_ref.1, f32[3,32]{1,0:T(4,128)} %base_hbm.1, f32[3,2048]{1,0:T(4,128)} %control_hbm.1, f32[2,3,2048]{2,1,0:T(4,128)} %copy.10.morph_hbm, s32[3,64]{1,0:T(4,128)} %corner_hbm.1, s32[1,64]{1,0:T(1,128)} %bitcast.4, s32[1,64]{1,0:T(1,128)} %bitcast.5, ...), custom_call_target="tpu_custom_call" | custom-call | tf_op jit(solution)/shard_map/pallas_call | solution.py:411
  13.9 0.0 copy-start
  13.9 1.4 %copy.13 = f32[1,64,128]{2,1,0:T(8,128)} copy(f32[1,64,128]{2,1,0:T(8,128)} %get-tuple-element.4) | data formatting | bytes 65536
  15.3 0.0 copy-done
  15.3 0.6 %copy.14 = f32[1,64,128]{2,1,0:T(8,128)} copy(f32[1,64,128]{2,1,0:T(8,128)S(1)} %copy-done) | data formatting | bytes 65536
Async XLA Ops:
  13.9 1.4 %copy-start = (f32[1,64,128]{2,1,0:T(8,128)S(1)}, f32[1,64,128]{2,1,0:T(8,128)}, u32[]{:S(2)}) copy-start(f32[1,64,128]{2,1,0:T(8,128)} %get-tuple-element.5) | copy-start | bytes 98308

commit v2 on v1

--- a/solution.py
+++ b/solution.py
@@ -194,6 +194,7 @@
 
 TILE_ROWS = 8
 LANES = 128
+LOAD_GRANT = 16 << 20
 FUSED_PANELS = 1024
 
 
@@ -230,7 +231,7 @@
     return centroid, weight, area
 
 
-def fused_kernel(
+def gather_kernel(
     panels_axis,
     cols_axis,
     order_ref,
@@ -241,8 +242,7 @@
     flag_hbm,
     owner_hbm,
     velocity_hbm,
-    shear_ref,
-    moment_ref,
+    gathered,
     base_ref,
     control_ref,
     morph_ref,
@@ -251,8 +251,6 @@
     owner_ref,
     velocity_ref,
     mix_ref,
-    gathered,
-    influence_ref,
     in_sem,
     send_sem,
     recv_sem,
@@ -263,7 +261,6 @@
     vert_dev = base_ref.shape[1]
     pan_dev = corner_ref.shape[1]
     loads = velocity_ref.shape[1]
-    panels_total = pan_dev * owners
 
     def peer_of(offset):
         peer = lax.rem(me + offset, owners)
@@ -293,12 +290,13 @@
     for fetch in fetches:
         fetch.wait()
 
-    mix_ref[0:3, 0:loads] = velocity_ref[...]
-    mix_ref[0:3, LANES : LANES + vert_dev] = base_ref[...]
+    mix_ref[0:3, 0:vert_dev] = base_ref[...]
     mixed = mix_ref[...].T
-    velocity_col = [mixed[0:loads, a : a + 1] for a in range(3)]
-    points_col = [mixed[LANES : LANES + vert_dev, a : a + 1] for a in range(3)]
-    weights = morph_ref[order_ref[lax.axis_index("phase")]]
+    points_col = [mixed[0:vert_dev, a : a + 1] for a in range(3)]
+    gathered[owners] = jnp.zeros((TILE_ROWS, LANES), jnp.float32)
+    gathered[owners, 0:3, 0:loads] = velocity_ref[...]
+    slot = order_ref[lax.axis_index("phase")]
+    weights = jnp.concatenate([morph_ref[a, pl.ds(slot, 1), :] for a in range(3)], axis=0)
     centroid, weight, area = own_geometry_rows(
         weights, points_col, corner_ref[...] - me * vert_dev, control_ref, vert_dev
     )
@@ -335,6 +333,16 @@
             device_id_type=pl.DeviceIdType.MESH,
         ).wait_recv()
 
+    for send in sends:
+        send.wait_send()
+
+
+def load_kernel(panels_axis, cols_axis, pan_dev, loads, gathered, shear_ref, moment_ref, influence_ref):
+    owners = panels_axis * cols_axis
+    me = lax.axis_index("panels") * cols_axis + lax.axis_index("cols")
+    panels_total = pan_dev * owners
+    spread = gathered[owners].T
+    velocity_col = [spread[0:loads, a : a + 1] for a in range(3)]
     rows = jnp.concatenate([gathered[d, :, 0:pan_dev] for d in range(owners)], axis=1)
     columns = rows.T
     kernel_scale = 1.0 / (4.0 * math.pi * math.sqrt(panels_total))
@@ -377,8 +385,6 @@
     moment_ref[0] = (summed[:, STATIONS : 2 * STATIONS] + summed[:, 2 * STATIONS :]) * (
         inv_root / (STATIONS * owners)
     )
-    for send in sends:
-        send.wait_send()
 
 
 def fused_shards(
@@ -400,31 +406,39 @@
     hbm_inputs = (
         base_points,
         control_points,
-        morph_weights,
+        morph_weights.transpose(1, 0, 2),
         connectivity,
         free_flags.reshape(1, pan_dev),
         station_owner.reshape(1, pan_dev),
         load_velocity.T,
     )
+    gathered = pl.pallas_call(
+        functools.partial(gather_kernel, panels_axis, cols_axis),
+        out_shape=pltpu.VMEM((owners + 1, TILE_ROWS, LANES), jnp.float32),
+        in_specs=[pl.BlockSpec(memory_space=pltpu.SMEM)]
+        + [pl.BlockSpec(memory_space=pltpu.HBM)] * len(hbm_inputs),
+        out_specs=pl.BlockSpec(memory_space=pltpu.VMEM),
+        scratch_shapes=[pltpu.VMEM(part.shape, part.dtype) for part in hbm_inputs]
+        + [
+            pltpu.VMEM((TILE_ROWS, LANES), jnp.float32),
+            pltpu.SemaphoreType.DMA((len(hbm_inputs),)),
+            pltpu.SemaphoreType.DMA((owners,)),
+            pltpu.SemaphoreType.DMA((owners,)),
+        ],
+        compiler_params=pltpu.CompilerParams(
+            collective_id=0, has_side_effects=True
+        ),
+    )(variant_order, *hbm_inputs)
     result = jax.ShapeDtypeStruct((1, loads, STATIONS), jnp.float32)
     return tuple(
         pl.pallas_call(
-            functools.partial(fused_kernel, panels_axis, cols_axis),
+            functools.partial(load_kernel, panels_axis, cols_axis, pan_dev, loads),
             out_shape=(result, result),
-            in_specs=[pl.BlockSpec(memory_space=pltpu.SMEM)]
-            + [pl.BlockSpec(memory_space=pltpu.HBM)] * len(hbm_inputs),
+            in_specs=[pl.BlockSpec(memory_space=pltpu.VMEM)],
             out_specs=(pl.BlockSpec(memory_space=pltpu.VMEM),) * 2,
-            scratch_shapes=[pltpu.VMEM(part.shape, part.dtype) for part in hbm_inputs]
-            + [
-                pltpu.VMEM((TILE_ROWS, 2 * LANES), jnp.float32),
-                pltpu.VMEM((owners, TILE_ROWS, LANES), jnp.float32),
-                pltpu.VMEM((panels_total, panels_total), jnp.bfloat16),
-                pltpu.SemaphoreType.DMA((len(hbm_inputs),)),
-                pltpu.SemaphoreType.DMA((owners,)),
-                pltpu.SemaphoreType.DMA((owners,)),
-            ],
-            compiler_params=pltpu.CompilerParams(collective_id=0, has_side_effects=True),
-        )(variant_order, *hbm_inputs)
+            scratch_shapes=[pltpu.VMEM((panels_total, panels_total), jnp.bfloat16)],
+            compiler_params=pltpu.CompilerParams(vmem_limit_bytes=LOAD_GRANT),
+        )(gathered)
     )
 
 

time: 16.2 us -> 12.6 us (0.78)
  local copies, waits for them, and re-layouts: 3.45 us -> 0 us
    unnamed x5 -> x0, local copies, waits for them, and re-layouts: 3.45 us -> none
    pallas_call x1 -> x2, Pallas kernels: 11.8 us -> 11.8 us  [the longest x1 9.91 us: fused_shards(): pl.pallas_call(functools.partial(gather_kernel, panels_axis, cols_axis),...]
where the time goes in v2:
time: 12.6 us; the launch traced here: 12.4 us
  Pallas kernels  11.8 us (94%)
  between operations  0.64 us (5%)
    pallas_call x1, Pallas kernels, fused_shards(): pl.pallas_call(functools.partial(gather_kernel, panels_axis, cols_axis),...  9.91 us
    pallas_call x1, Pallas kernels, fused_shards(): pl.pallas_call(functools.partial(load_kernel, panels_axis, cols_axis, pan...  1.89 us

profile of v2, /device:TPU:0, one launch (start us, length us, event | category | flops | bytes accessed | tf_op | source)
XLA Modules:
  0.0 12.4 jit_solution(1880943215099878010)
XLA Ops:
  0.6 9.9 %shard_map.95.gathered = f32[9,8,128]{2,1,0:T(8,128)S(1)} custom-call(s32[2]{0:T(128)} %order_ref.1, f32[3,32]{1,0:T(4,128)} %base_hbm.1, f32[3,2048]{1,0:T(4,128)} %control_hbm.1, f32[3,2,2048]{2,1,0:T(2,128)} %bitcast.4, s32[3,64]{1,0:T(4,128)} %corner_hbm.1, s32[1,64]{1,0:T(1,128)} %bitcast.6, s32[1,64]{1,0:T(1,128)} %bitcast.7, f32[3,64]{1,0:T(4,128)} %bitcast.5), custom_call_target="tpu_custom_call" | custom-call | tf_op jit(solution)/shard_map/pallas_call | solution.py:415
  10.6 1.9 %shard_map.96 = (f32[1,64,128]{2,1,0:T(8,128)}, f32[1,64,128]{2,1,0:T(8,128)}) custom-call(f32[9,8,128]{2,1,0:T(8,128)S(1)} %shard_map.95.gathered), custom_call_target="tpu_custom_call" | custom-call | tf_op jit(solution)/shard_map/pallas_call | solution.py:434

commit v3 on v2

--- a/solution.py
+++ b/solution.py
@@ -193,6 +193,7 @@
 
 
 TILE_ROWS = 8
+HALF_ROWS = 4
 LANES = 128
 LOAD_GRANT = 16 << 20
 FUSED_PANELS = 1024
@@ -234,7 +235,7 @@
 def gather_kernel(
     panels_axis,
     cols_axis,
-    order_ref,
+    order_hbm,
     base_hbm,
     control_hbm,
     morph_hbm,
@@ -243,6 +244,8 @@
     owner_hbm,
     velocity_hbm,
     gathered,
+    influence_ref,
+    order_ref,
     base_ref,
     control_ref,
     morph_ref,
@@ -251,6 +254,7 @@
     owner_ref,
     velocity_ref,
     mix_ref,
+    spread_ref,
     in_sem,
     send_sem,
     recv_sem,
@@ -261,19 +265,12 @@
     vert_dev = base_ref.shape[1]
     pan_dev = corner_ref.shape[1]
     loads = velocity_ref.shape[1]
-
-    def peer_of(offset):
-        peer = lax.rem(me + offset, owners)
-        return {"panels": peer // cols_axis, "cols": lax.rem(peer, cols_axis)}
-
-    barrier = pltpu.get_barrier_semaphore()
-    for offset in range(1, owners):
-        pl.semaphore_signal(
-            barrier, inc=1, device_id=peer_of(offset), device_id_type=pl.DeviceIdType.MESH
-        )
+    panels_total = pan_dev * owners
+
     pairs = (
         (base_hbm, base_ref),
         (control_hbm, control_ref),
+        (order_hbm, order_ref),
         (morph_hbm, morph_ref),
         (corner_hbm, corner_ref),
         (flag_hbm, flag_ref),
@@ -286,6 +283,14 @@
     ]
     for fetch in fetches:
         fetch.start()
+    steps = [(r, c) for r in range(panels_axis) for c in range(cols_axis)][::-1][:-1]
+    peers = [
+        {"panels": lax.rem(row + r, panels_axis), "cols": lax.rem(col + c, cols_axis)}
+        for r, c in steps
+    ]
+    barrier = pltpu.get_barrier_semaphore()
+    for peer in peers:
+        pl.semaphore_signal(barrier, inc=1, device_id=peer, device_id_type=pl.DeviceIdType.MESH)
     mix_ref[...] = jnp.zeros(mix_ref.shape, jnp.float32)
     for fetch in fetches:
         fetch.wait()
@@ -293,7 +298,7 @@
     mix_ref[0:3, 0:vert_dev] = base_ref[...]
     mixed = mix_ref[...].T
     points_col = [mixed[0:vert_dev, a : a + 1] for a in range(3)]
-    gathered[owners] = jnp.zeros((TILE_ROWS, LANES), jnp.float32)
+    gathered[owners] = jnp.zeros((HALF_ROWS, LANES), jnp.float32)
     gathered[owners, 0:3, 0:loads] = velocity_ref[...]
     slot = order_ref[lax.axis_index("phase")]
     weights = jnp.concatenate([morph_ref[a, pl.ds(slot, 1), :] for a in range(3)], axis=0)
@@ -306,70 +311,99 @@
         + lax.rem(me * pan_dev, STATIONS)
         + lax.broadcasted_iota(jnp.int32, (1, pan_dev), 1)
     ).astype(jnp.float32)
-    rows = centroid + [weight] + [part * hull for part in area] + [station]
-    gathered[me, :, 0:pan_dev] = jnp.concatenate(rows, axis=0)
+    upper = jnp.concatenate(centroid + [weight], axis=0)
+    lower = jnp.concatenate([part * hull for part in area] + [station], axis=0)
+    gathered[me] = jnp.concatenate([upper, lower], axis=1)
 
     pl.semaphore_wait(barrier, owners - 1)
     sends = []
-    for offset in range(1, owners):
+    for k, peer in enumerate(peers):
         send = pltpu.make_async_remote_copy(
             src_ref=gathered.at[me],
             dst_ref=gathered.at[me],
-            send_sem=send_sem.at[offset - 1],
+            send_sem=send_sem.at[k],
             recv_sem=recv_sem.at[me],
-            device_id=peer_of(offset),
+            device_id=peer,
             device_id_type=pl.DeviceIdType.MESH,
         )
         send.start()
         sends.append(send)
-    for offset in range(1, owners):
-        source = lax.rem(me + offset, owners)
-        pltpu.make_async_remote_copy(
-            src_ref=gathered.at[source],
-            dst_ref=gathered.at[source],
-            send_sem=send_sem.at[offset - 1],
-            recv_sem=recv_sem.at[source],
-            device_id=peer_of(offset),
-            device_id_type=pl.DeviceIdType.MESH,
-        ).wait_recv()
-
+
+    kernel_scale = 1.0 / (4.0 * math.pi * math.sqrt(panels_total))
+    tiles = panels_total // LANES
+    per_tile = owners // tiles
+    block = 32
+
+    def fill(target_row, source_tile):
+        for start in range(0, LANES, block):
+            at = source_tile * LANES + start
+            span = slice(at, at + block)
+            dx = target_row[0:1] - spread_ref[0, span, :]
+            dy = target_row[1:2] - spread_ref[1, span, :]
+            dz = target_row[2:3] - spread_ref[2, span, :]
+            distance = dx * dx + dy * dy + dz * dz
+            yield span, (spread_ref[3, span, :] * lax.rsqrt(distance + CORE_SQUARE)).astype(
+                jnp.bfloat16
+            )
+
+    tile_rows = []
+    for tile in range(tiles):
+        for source in range(tile * per_tile, (tile + 1) * per_tile):
+
+            @pl.when(me != source)
+            def _():
+                pltpu.make_async_remote_copy(
+                    src_ref=gathered.at[source],
+                    dst_ref=gathered.at[source],
+                    send_sem=send_sem.at[0],
+                    recv_sem=recv_sem.at[source],
+                    device_id=peers[0],
+                    device_id_type=pl.DeviceIdType.MESH,
+                ).wait_recv()
+
+        own = jnp.concatenate(
+            [gathered[tile * per_tile + d, :, 0:pan_dev] for d in range(per_tile)], axis=1
+        )
+        tile_rows.append(own)
+        lanes = slice(tile * LANES, (tile + 1) * LANES)
+        for before in range(tile):
+            for span, value in fill(own, before):
+                influence_ref[span, lanes] = value
+        columns = jnp.concatenate([own, own], axis=0).T
+        for a in range(4):
+            column = columns[:, a : a + 1] * kernel_scale if a == 3 else columns[:, a : a + 1]
+            spread_ref[a, lanes, :] = jnp.broadcast_to(column, (LANES, LANES))
+        for target in range(tile + 1):
+            for span, value in fill(tile_rows[target], tile):
+                influence_ref[span, target * LANES : (target + 1) * LANES] = value
     for send in sends:
         send.wait_send()
 
 
-def load_kernel(panels_axis, cols_axis, pan_dev, loads, gathered, shear_ref, moment_ref, influence_ref):
+def load_kernel(
+    panels_axis, cols_axis, pan_dev, loads, gathered, influence_ref, shear_ref, moment_ref
+):
     owners = panels_axis * cols_axis
     me = lax.axis_index("panels") * cols_axis + lax.axis_index("cols")
     panels_total = pan_dev * owners
-    spread = gathered[owners].T
+    spread = jnp.concatenate([gathered[owners], gathered[owners]], axis=0).T
     velocity_col = [spread[0:loads, a : a + 1] for a in range(3)]
-    rows = jnp.concatenate([gathered[d, :, 0:pan_dev] for d in range(owners)], axis=1)
-    columns = rows.T
-    kernel_scale = 1.0 / (4.0 * math.pi * math.sqrt(panels_total))
-    block = 32
-    for start in range(0, panels_total, block):
-        part = columns[start : start + block]
-        dx = rows[0:1] - part[:, 0:1]
-        dy = rows[1:2] - part[:, 1:2]
-        dz = rows[2:3] - part[:, 2:3]
-        distance = dx * dx + dy * dy + dz * dz
-        influence_ref[start : start + block, :] = (
-            (part[:, 3:4] * kernel_scale) * lax.rsqrt(distance + CORE_SQUARE)
-        ).astype(jnp.bfloat16)
+    rows = jnp.concatenate([gathered[d, :, pan_dev : 2 * pan_dev] for d in range(owners)], axis=1)
+    columns = jnp.concatenate([rows, rows], axis=0).T
     boundary = (
-        velocity_col[0] * rows[4:5] + velocity_col[1] * rows[5:6] + velocity_col[2] * rows[6:7]
+        velocity_col[0] * rows[0:1] + velocity_col[1] * rows[1:2] + velocity_col[2] * rows[2:3]
     )
     first = boundary.astype(jnp.bfloat16)
     induced = jnp.dot(first, influence_ref[...], preferred_element_type=jnp.float32)
     second = (first.astype(jnp.float32) + (boundary - induced)).astype(jnp.bfloat16)
     pressure = jnp.dot(second, influence_ref[...], preferred_element_type=jnp.float32)
-    force = pressure * rows[6:7]
+    force = pressure * rows[2:3]
     force_high = force.astype(jnp.bfloat16)
     force_low = (force - force_high.astype(jnp.float32)).astype(jnp.bfloat16)
     here = (
         me * STATIONS + lax.broadcasted_iota(jnp.int32, (panels_total, STATIONS), 1)
     ).astype(jnp.float32)
-    gap = here - columns[:, 7:8]
+    gap = here - columns[:, 3:4]
     reached = jnp.where(gap >= 0.0, 1.0, 0.0).astype(jnp.bfloat16)
     arm = jnp.maximum(gap, 0.0)
     arm_high = arm.astype(jnp.bfloat16)
@@ -404,6 +438,7 @@
     loads = load_velocity.shape[0]
     panels_total = pan_dev * owners
     hbm_inputs = (
+        variant_order,
         base_points,
         control_points,
         morph_weights.transpose(1, 0, 2),
@@ -412,15 +447,19 @@
         station_owner.reshape(1, pan_dev),
         load_velocity.T,
     )
-    gathered = pl.pallas_call(
+    gathered, influence = pl.pallas_call(
         functools.partial(gather_kernel, panels_axis, cols_axis),
-        out_shape=pltpu.VMEM((owners + 1, TILE_ROWS, LANES), jnp.float32),
-        in_specs=[pl.BlockSpec(memory_space=pltpu.SMEM)]
-        + [pl.BlockSpec(memory_space=pltpu.HBM)] * len(hbm_inputs),
-        out_specs=pl.BlockSpec(memory_space=pltpu.VMEM),
-        scratch_shapes=[pltpu.VMEM(part.shape, part.dtype) for part in hbm_inputs]
+        out_shape=(
+            pltpu.VMEM((owners + 1, HALF_ROWS, LANES), jnp.float32),
+            pltpu.VMEM((panels_total, panels_total), jnp.bfloat16),
+        ),
+        in_specs=[pl.BlockSpec(memory_space=pltpu.HBM)] * len(hbm_inputs),
+        out_specs=(pl.BlockSpec(memory_space=pltpu.VMEM),) * 2,
+        scratch_shapes=[pltpu.SMEM(variant_order.shape, variant_order.dtype)]
+        + [pltpu.VMEM(part.shape, part.dtype) for part in hbm_inputs[1:]]
         + [
             pltpu.VMEM((TILE_ROWS, LANES), jnp.float32),
+            pltpu.VMEM((HALF_ROWS, panels_total, LANES), jnp.float32),
             pltpu.SemaphoreType.DMA((len(hbm_inputs),)),
             pltpu.SemaphoreType.DMA((owners,)),
             pltpu.SemaphoreType.DMA((owners,)),
@@ -428,17 +467,16 @@
         compiler_params=pltpu.CompilerParams(
             collective_id=0, has_side_effects=True
         ),
-    )(variant_order, *hbm_inputs)
+    )(*hbm_inputs)
     result = jax.ShapeDtypeStruct((1, loads, STATIONS), jnp.float32)
     return tuple(
         pl.pallas_call(
             functools.partial(load_kernel, panels_axis, cols_axis, pan_dev, loads),
             out_shape=(result, result),
-            in_specs=[pl.BlockSpec(memory_space=pltpu.VMEM)],
+            in_specs=[pl.BlockSpec(memory_space=pltpu.VMEM)] * 2,
             out_specs=(pl.BlockSpec(memory_space=pltpu.VMEM),) * 2,
-            scratch_shapes=[pltpu.VMEM((panels_total, panels_total), jnp.bfloat16)],
             compiler_params=pltpu.CompilerParams(vmem_limit_bytes=LOAD_GRANT),
-        )(gathered)
+        )(gathered, influence)
     )
 
 
@@ -454,8 +492,9 @@
     pan_dev = connectivity.shape[1]
     fits = (
         pan_dev * owners <= FUSED_PANELS
-        and pan_dev <= LANES
+        and LANES == 2 * pan_dev
         and STATIONS % pan_dev == 0
+        and owners % 2 == 0
         and base_points.shape[1] <= LANES
         and load_velocity.shape[0] <= LANES
         and variant_order.shape[0] == mesh.shape["phase"]

time: 12.6 us -> 12.1 us (0.960)
  Pallas kernels: 11.8 us -> 11.3 us
    pallas_call x1, Pallas kernels: 1.89 us -> 1.37 us  [fused_shards(): pl.pallas_call(functools.partial(load_kernel, panels_axis, cols_axis, pan...]
where the time goes in v3:
time: 12.1 us; the launch traced here: 11.9 us
  Pallas kernels  11.3 us (93%)
  between operations  0.64 us (5%)
    pallas_call x1, Pallas kernels, fused_shards(): pl.pallas_call(functools.partial(gather_kernel, panels_axis, cols_axis),...  9.93 us
    pallas_call x1, Pallas kernels, fused_shards(): pl.pallas_call(functools.partial(load_kernel, panels_axis, cols_axis, pan...  1.37 us

profile of v3, /device:TPU:0, one launch (start us, length us, event | category | flops | bytes accessed | tf_op | source)
XLA Modules:
  0.0 11.9 jit_solution(6569632265497965625)
XLA Ops:
  0.6 9.9 %shard_map.95 = (f32[9,4,128]{2,1,0:T(4,128)S(1)}, bf16[512,512]{1,0:T(8,128)(2,1)S(1)}) custom-call(s32[2]{0:T(128)} %order_hbm.1, f32[3,32]{1,0:T(4,128)} %base_hbm.1, f32[3,2048]{1,0:T(4,128)} %control_hbm.1, f32[3,2,2048]{2,1,0:T(2,128)} %bitcast.4, s32[3,64]{1,0:T(4,128)} %corner_hbm.1, s32[1,64]{1,0:T(1,128)} %bitcast.6, s32[1,64]{1,0:T(1,128)} %bitcast.7, ...), custom_call_target="tpu_custom_call" | custom-call | tf_op jit(solution)/shard_map/pallas_call | solution.py:450
  10.6 1.4 %shard_map.96 = (f32[1,64,128]{2,1,0:T(8,128)}, f32[1,64,128]{2,1,0:T(8,128)}) custom-call(f32[9,4,128]{2,1,0:T(4,128)S(1)} %get-tuple-element.4.gathered, bf16[512,512]{1,0:T(8,128)(2,1)S(1)} %get-tuple-element.5.influence_ref), custom_call_target="tpu_custom_call" | custom-call | tf_op jit(solution)/shard_map/pallas_call | solution.py:473

commit v4 on v3

--- a/solution.py
+++ b/solution.py
@@ -199,19 +199,22 @@
 FUSED_PANELS = 1024
 
 
-def own_geometry_rows(weights, points_col, corner_rows, control_ref, vert_dev):
+def own_geometry_rows(weights_of, points_col, corner_rows_of, control_ref, vert_dev, before_chunk):
     controls = control_ref.shape[1]
     chunk = min(controls, 2 * LANES)
     totals = [jnp.zeros((vert_dev, chunk), jnp.float32) for _ in range(3)]
     columns = [jnp.broadcast_to(col, (vert_dev, chunk)) for col in points_col]
     for start in range(0, controls, chunk):
         span = slice(start, start + chunk)
+        before_chunk(start)
+        weights = weights_of(span)
         dx = control_ref[0:1, span] - columns[0]
         dy = control_ref[1:2, span] - columns[1]
         dz = control_ref[2:3, span] - columns[2]
         basis = lax.rsqrt(1.0 + (dx * dx + dy * dy + dz * dz))
-        totals = [totals[a] + weights[a : a + 1, span] * basis for a in range(3)]
+        totals = [totals[a] + weights[a] * basis for a in range(3)]
     moved = [points_col[a] + jnp.sum(totals[a], axis=1, keepdims=True) for a in range(3)]
+    corner_rows = corner_rows_of()
     vertex = lax.broadcasted_iota(jnp.int32, (vert_dev, corner_rows.shape[1]), 0)
     corners = []
     for q in range(3):
@@ -243,8 +246,10 @@
     flag_hbm,
     owner_hbm,
     velocity_hbm,
-    gathered,
     influence_ref,
+    masks_ref,
+    boundary_ref,
+    lift_ref,
     order_ref,
     base_ref,
     control_ref,
@@ -255,6 +260,7 @@
     velocity_ref,
     mix_ref,
     spread_ref,
+    gathered,
     in_sem,
     send_sem,
     recv_sem,
@@ -267,23 +273,32 @@
     loads = velocity_ref.shape[1]
     panels_total = pan_dev * owners
 
-    pairs = (
-        (base_hbm, base_ref),
-        (control_hbm, control_ref),
-        (order_hbm, order_ref),
-        (morph_hbm, morph_ref),
+    halves = 2
+    wide = control_ref.shape[1] // halves
+    pairs = [(base_hbm, base_ref), (order_hbm, order_ref)]
+    for half in range(halves):
+        span = pl.ds(half * wide, wide)
+        pairs += [
+            (control_hbm.at[:, span], control_ref.at[:, span]),
+            (morph_hbm.at[:, :, span], morph_ref.at[:, :, span]),
+        ]
+    pairs += [
         (corner_hbm, corner_ref),
         (flag_hbm, flag_ref),
         (owner_hbm, owner_ref),
         (velocity_hbm, velocity_ref),
-    )
+    ]
     fetches = [
         pltpu.make_async_copy(source, target, in_sem.at[k])
         for k, (source, target) in enumerate(pairs)
     ]
     for fetch in fetches:
         fetch.start()
-    steps = [(r, c) for r in range(panels_axis) for c in range(cols_axis)][::-1][:-1]
+    steps = [
+        (r % panels_axis, c)
+        for r in range(1, panels_axis + 1)
+        for c in reversed(range(cols_axis))
+    ][:-1]
     peers = [
         {"panels": lax.rem(row + r, panels_axis), "cols": lax.rem(col + c, cols_axis)}
         for r, c in steps
@@ -292,18 +307,37 @@
     for peer in peers:
         pl.semaphore_signal(barrier, inc=1, device_id=peer, device_id_type=pl.DeviceIdType.MESH)
     mix_ref[...] = jnp.zeros(mix_ref.shape, jnp.float32)
-    for fetch in fetches:
-        fetch.wait()
-
+    fetches[0].wait()
     mix_ref[0:3, 0:vert_dev] = base_ref[...]
     mixed = mix_ref[...].T
     points_col = [mixed[0:vert_dev, a : a + 1] for a in range(3)]
-    gathered[owners] = jnp.zeros((HALF_ROWS, LANES), jnp.float32)
-    gathered[owners, 0:3, 0:loads] = velocity_ref[...]
+    fetches[1].wait()
     slot = order_ref[lax.axis_index("phase")]
-    weights = jnp.concatenate([morph_ref[a, pl.ds(slot, 1), :] for a in range(3)], axis=0)
+
+    def before_chunk(start):
+        if start % wide == 0:
+            for part in range(2):
+                fetches[2 + 2 * (start // wide) + part].wait()
+
+    def weights_of(span):
+        picked = [morph_ref[a, 0:1, span] for a in range(3)]
+        for v in range(1, morph_ref.shape[1]):
+            other = [morph_ref[a, v : v + 1, span] for a in range(3)]
+            picked = [jnp.where(slot == v, new, old) for new, old in zip(other, picked)]
+        return picked
+
+    def corner_rows_of():
+        for fetch in fetches[-4:]:
+            fetch.wait()
+        return corner_ref[...] - me * vert_dev
+
     centroid, weight, area = own_geometry_rows(
-        weights, points_col, corner_ref[...] - me * vert_dev, control_ref, vert_dev
+        weights_of,
+        points_col,
+        corner_rows_of,
+        control_ref,
+        vert_dev,
+        before_chunk,
     )
     hull = (1 - flag_ref[...]).astype(jnp.float32)
     station = (
@@ -329,6 +363,12 @@
         send.start()
         sends.append(send)
 
+    mix_ref[0:3, 0:loads] = velocity_ref[...]
+    velocity = mix_ref[...].T
+    velocity_col = [velocity[0:loads, a : a + 1] for a in range(3)]
+    here = (me * STATIONS + lax.broadcasted_iota(jnp.int32, (LANES, STATIONS), 1)).astype(
+        jnp.float32
+    )
     kernel_scale = 1.0 / (4.0 * math.pi * math.sqrt(panels_total))
     tiles = panels_total // LANES
     per_tile = owners // tiles
@@ -361,56 +401,50 @@
                     device_id_type=pl.DeviceIdType.MESH,
                 ).wait_recv()
 
-        own = jnp.concatenate(
-            [gathered[tile * per_tile + d, :, 0:pan_dev] for d in range(per_tile)], axis=1
+        blocks = [gathered[tile * per_tile + d] for d in range(per_tile)]
+        own = jnp.concatenate([part[:, 0:pan_dev] for part in blocks], axis=1)
+        load = jnp.concatenate([part[:, pan_dev : 2 * pan_dev] for part in blocks], axis=1)
+        tile_rows.append(own)
+        columns = jnp.concatenate([own, load], axis=0).T
+        lanes = slice(tile * LANES, (tile + 1) * LANES)
+        boundary_ref[:, lanes] = (
+            velocity_col[0] * load[0:1] + velocity_col[1] * load[1:2] + velocity_col[2] * load[2:3]
         )
-        tile_rows.append(own)
-        lanes = slice(tile * LANES, (tile + 1) * LANES)
+        lift_ref[:, lanes] = load[2:3]
         for before in range(tile):
             for span, value in fill(own, before):
                 influence_ref[span, lanes] = value
-        columns = jnp.concatenate([own, own], axis=0).T
         for a in range(4):
             column = columns[:, a : a + 1] * kernel_scale if a == 3 else columns[:, a : a + 1]
             spread_ref[a, lanes, :] = jnp.broadcast_to(column, (LANES, LANES))
         for target in range(tile + 1):
             for span, value in fill(tile_rows[target], tile):
                 influence_ref[span, target * LANES : (target + 1) * LANES] = value
+        gap = here - columns[:, 7:8]
+        arm = jnp.maximum(gap, 0.0)
+        arm_high = arm.astype(jnp.bfloat16)
+        masks_ref[lanes, 0:STATIONS] = jnp.where(gap >= 0.0, 1.0, 0.0).astype(jnp.bfloat16)
+        masks_ref[lanes, STATIONS : 2 * STATIONS] = arm_high
+        masks_ref[lanes, 2 * STATIONS :] = (arm - arm_high.astype(jnp.float32)).astype(
+            jnp.bfloat16
+        )
     for send in sends:
         send.wait_send()
 
 
-def load_kernel(
-    panels_axis, cols_axis, pan_dev, loads, gathered, influence_ref, shear_ref, moment_ref
-):
-    owners = panels_axis * cols_axis
-    me = lax.axis_index("panels") * cols_axis + lax.axis_index("cols")
-    panels_total = pan_dev * owners
-    spread = jnp.concatenate([gathered[owners], gathered[owners]], axis=0).T
-    velocity_col = [spread[0:loads, a : a + 1] for a in range(3)]
-    rows = jnp.concatenate([gathered[d, :, pan_dev : 2 * pan_dev] for d in range(owners)], axis=1)
-    columns = jnp.concatenate([rows, rows], axis=0).T
-    boundary = (
-        velocity_col[0] * rows[0:1] + velocity_col[1] * rows[1:2] + velocity_col[2] * rows[2:3]
-    )
+def load_kernel(owners, influence_ref, masks_ref, boundary_ref, lift_ref, shear_ref, moment_ref):
+    loads, panels_total = boundary_ref.shape
+    boundary = boundary_ref[...]
     first = boundary.astype(jnp.bfloat16)
     induced = jnp.dot(first, influence_ref[...], preferred_element_type=jnp.float32)
     second = (first.astype(jnp.float32) + (boundary - induced)).astype(jnp.bfloat16)
     pressure = jnp.dot(second, influence_ref[...], preferred_element_type=jnp.float32)
-    force = pressure * rows[2:3]
+    force = pressure * lift_ref[...]
     force_high = force.astype(jnp.bfloat16)
     force_low = (force - force_high.astype(jnp.float32)).astype(jnp.bfloat16)
-    here = (
-        me * STATIONS + lax.broadcasted_iota(jnp.int32, (panels_total, STATIONS), 1)
-    ).astype(jnp.float32)
-    gap = here - columns[:, 3:4]
-    reached = jnp.where(gap >= 0.0, 1.0, 0.0).astype(jnp.bfloat16)
-    arm = jnp.maximum(gap, 0.0)
-    arm_high = arm.astype(jnp.bfloat16)
-    arm_low = (arm - arm_high.astype(jnp.float32)).astype(jnp.bfloat16)
     summed = jnp.dot(
         jnp.concatenate([force_high, force_low], axis=0),
-        jnp.concatenate([reached, arm_high, arm_low], axis=1),
+        masks_ref[...],
         preferred_element_type=jnp.float32,
     )
     summed = summed[0:loads] + summed[loads : 2 * loads]
@@ -447,20 +481,23 @@
         station_owner.reshape(1, pan_dev),
         load_velocity.T,
     )
-    gathered, influence = pl.pallas_call(
+    parts = pl.pallas_call(
         functools.partial(gather_kernel, panels_axis, cols_axis),
         out_shape=(
-            pltpu.VMEM((owners + 1, HALF_ROWS, LANES), jnp.float32),
             pltpu.VMEM((panels_total, panels_total), jnp.bfloat16),
+            pltpu.VMEM((panels_total, 3 * STATIONS), jnp.bfloat16),
+            pltpu.VMEM((loads, panels_total), jnp.float32),
+            pltpu.VMEM((1, panels_total), jnp.float32),
         ),
         in_specs=[pl.BlockSpec(memory_space=pltpu.HBM)] * len(hbm_inputs),
-        out_specs=(pl.BlockSpec(memory_space=pltpu.VMEM),) * 2,
+        out_specs=(pl.BlockSpec(memory_space=pltpu.VMEM),) * 4,
         scratch_shapes=[pltpu.SMEM(variant_order.shape, variant_order.dtype)]
         + [pltpu.VMEM(part.shape, part.dtype) for part in hbm_inputs[1:]]
         + [
             pltpu.VMEM((TILE_ROWS, LANES), jnp.float32),
             pltpu.VMEM((HALF_ROWS, panels_total, LANES), jnp.float32),
-            pltpu.SemaphoreType.DMA((len(hbm_inputs),)),
+            pltpu.VMEM((owners, HALF_ROWS, LANES), jnp.float32),
+            pltpu.SemaphoreType.DMA((len(hbm_inputs) + 2,)),
             pltpu.SemaphoreType.DMA((owners,)),
             pltpu.SemaphoreType.DMA((owners,)),
         ],
@@ -471,12 +508,12 @@
     result = jax.ShapeDtypeStruct((1, loads, STATIONS), jnp.float32)
     return tuple(
         pl.pallas_call(
-            functools.partial(load_kernel, panels_axis, cols_axis, pan_dev, loads),
+            functools.partial(load_kernel, owners),
             out_shape=(result, result),
-            in_specs=[pl.BlockSpec(memory_space=pltpu.VMEM)] * 2,
+            in_specs=[pl.BlockSpec(memory_space=pltpu.VMEM)] * 4,
             out_specs=(pl.BlockSpec(memory_space=pltpu.VMEM),) * 2,
             compiler_params=pltpu.CompilerParams(vmem_limit_bytes=LOAD_GRANT),
-        )(gathered, influence)
+        )(*parts)
     )
 
 

time: 12.1 us -> 12 us (level)
    pallas_call x1, Pallas kernels: 1.37 us -> 1.19 us  [fused_shards(): pl.pallas_call(functools.partial(load_kernel, owners), out_shape=(result,...]
where the time goes in v4:
time: 12 us; the launch traced here: 11.8 us
  Pallas kernels  11.2 us (93%)
  between operations  0.64 us (5%)
    pallas_call x1, Pallas kernels, fused_shards(): pl.pallas_call(functools.partial(gather_kernel, panels_axis, cols_axis),...  9.97 us
    pallas_call x1, Pallas kernels, fused_shards(): pl.pallas_call(functools.partial(load_kernel, owners), out_shape=(result,...  1.19 us

profile of v4, /device:TPU:0, one launch (start us, length us, event | category | flops | bytes accessed | tf_op | source)
XLA Modules:
  0.0 11.8 jit_solution(11908244025970875693)
XLA Ops:
  0.6 10.0 %shard_map.95 = (bf16[512,512]{1,0:T(8,128)(2,1)S(1)}, bf16[512,384]{1,0:T(8,128)(2,1)S(1)}, f32[64,512]{1,0:T(8,128)S(1)}, f32[1,512]{1,0:T(1,128)S(1)}) custom-call(s32[2]{0:T(128)} %order_hbm.1, f32[3,32]{1,0:T(4,128)} %base_hbm.1, f32[3,2048]{1,0:T(4,128)} %control_hbm.1, f32[3,2,2048]{2,1,0:T(2,128)} %bitcast.4, s32[3,64]{1,0:T(4,128)} %corner_hbm.1, ...), custom_call_target="tpu_custom_call" | custom-call | tf_op jit(solution)/shard_map/pallas_call | solution.py:484
  10.6 1.2 %shard_map.96 = (f32[1,64,128]{2,1,0:T(8,128)}, f32[1,64,128]{2,1,0:T(8,128)}) custom-call(bf16[512,512]{1,0:T(8,128)(2,1)S(1)} %get-tuple-element.6.influence_ref, bf16[512,384]{1,0:T(8,128)(2,1)S(1)} %get-tuple-element.7.masks_ref, f32[64,512]{1,0:T(8,128)S(1)} %get-tuple-element.8.boundary_ref, f32[1,512]{1,0:T(1,128)S(1)} %get-tuple-element.9.lift_ref), custom_call_target="tpu_custom_call" | custom-call | tf_op jit(solution)/shard_map/pallas_call | solution.py:510

commit v5 on v4

--- a/solution.py
+++ b/solution.py
@@ -374,17 +374,12 @@
     per_tile = owners // tiles
     block = 32
 
-    def fill(target_row, source_tile):
-        for start in range(0, LANES, block):
-            at = source_tile * LANES + start
-            span = slice(at, at + block)
-            dx = target_row[0:1] - spread_ref[0, span, :]
-            dy = target_row[1:2] - spread_ref[1, span, :]
-            dz = target_row[2:3] - spread_ref[2, span, :]
-            distance = dx * dx + dy * dy + dz * dz
-            yield span, (spread_ref[3, span, :] * lax.rsqrt(distance + CORE_SQUARE)).astype(
-                jnp.bfloat16
-            )
+    def influence_of(target_row, source):
+        dx = target_row[0:1] - source[0]
+        dy = target_row[1:2] - source[1]
+        dz = target_row[2:3] - source[2]
+        distance = dx * dx + dy * dy + dz * dz
+        return (source[3] * lax.rsqrt(distance + CORE_SQUARE)).astype(jnp.bfloat16)
 
     tile_rows = []
     for tile in range(tiles):
@@ -411,15 +406,21 @@
             velocity_col[0] * load[0:1] + velocity_col[1] * load[1:2] + velocity_col[2] * load[2:3]
         )
         lift_ref[:, lanes] = load[2:3]
-        for before in range(tile):
-            for span, value in fill(own, before):
-                influence_ref[span, lanes] = value
+        for start in range(0, tile * LANES, block):
+            span = slice(start, start + block)
+            influence_ref[span, lanes] = influence_of(
+                own, [spread_ref[a, span, :] for a in range(4)]
+            )
         for a in range(4):
             column = columns[:, a : a + 1] * kernel_scale if a == 3 else columns[:, a : a + 1]
             spread_ref[a, lanes, :] = jnp.broadcast_to(column, (LANES, LANES))
-        for target in range(tile + 1):
-            for span, value in fill(tile_rows[target], tile):
-                influence_ref[span, target * LANES : (target + 1) * LANES] = value
+        for start in range(0, LANES, block):
+            span = slice(tile * LANES + start, tile * LANES + start + block)
+            source = [spread_ref[a, span, :] for a in range(4)]
+            for target in range(tile + 1):
+                influence_ref[span, target * LANES : (target + 1) * LANES] = influence_of(
+                    tile_rows[target], source
+                )
         gap = here - columns[:, 7:8]
         arm = jnp.maximum(gap, 0.0)
         arm_high = arm.astype(jnp.bfloat16)

time: 12 us -> 12 us (level)
  no operation moved by 1% of the time
where the time goes in v5:
time: 12 us; the launch traced here: 11.8 us
  Pallas kernels  11.2 us (93%)
  between operations  0.64 us (5%)
    pallas_call x1, Pallas kernels, fused_shards(): pl.pallas_call(functools.partial(gather_kernel, panels_axis, cols_axis),...  9.97 us
    pallas_call x1, Pallas kernels, fused_shards(): pl.pallas_call(functools.partial(load_kernel, owners), out_shape=(result,...  1.19 us

profile of v5, /device:TPU:0, one launch (start us, length us, event | category | flops | bytes accessed | tf_op | source)
XLA Modules:
  0.0 11.8 jit_solution(11908244025970875693)
XLA Ops:
  0.6 10.0 %shard_map.95 = (bf16[512,512]{1,0:T(8,128)(2,1)S(1)}, bf16[512,384]{1,0:T(8,128)(2,1)S(1)}, f32[64,512]{1,0:T(8,128)S(1)}, f32[1,512]{1,0:T(1,128)S(1)}) custom-call(s32[2]{0:T(128)} %order_hbm.1, f32[3,32]{1,0:T(4,128)} %base_hbm.1, f32[3,2048]{1,0:T(4,128)} %control_hbm.1, f32[3,2,2048]{2,1,0:T(2,128)} %bitcast.4, s32[3,64]{1,0:T(4,128)} %corner_hbm.1, ...), custom_call_target="tpu_custom_call" | custom-call | tf_op jit(solution)/shard_map/pallas_call | solution.py:485
  10.6 1.2 %shard_map.96 = (f32[1,64,128]{2,1,0:T(8,128)}, f32[1,64,128]{2,1,0:T(8,128)}) custom-call(bf16[512,512]{1,0:T(8,128)(2,1)S(1)} %get-tuple-element.6.influence_ref, bf16[512,384]{1,0:T(8,128)(2,1)S(1)} %get-tuple-element.7.masks_ref, f32[64,512]{1,0:T(8,128)S(1)} %get-tuple-element.8.boundary_ref, f32[1,512]{1,0:T(1,128)S(1)} %get-tuple-element.9.lift_ref), custom_call_target="tpu_custom_call" | custom-call | tf_op jit(solution)/shard_map/pallas_call | solution.py:511
